TPU v7x, 256 devices: a whole 4x4x8 slice. The times are simulated.
256 devices in a mesh: rows: 4 (over y), cand: 64 (over x, z, core).
Axes of the slice: x: 4, y: 4, z: 8, core: 2. Of those that a mesh axis runs over, the one named last changes fastest.
Arguments:
- whitened: float32 [256, 2048], P('cand', 'rows'), may hold values from -6 to 6
- factor_rows: float32 [2048, 2048], P('rows'), as said below
- diag_inv: float32 [2048, 512], P('rows'), as said below
- observed: float32 [22, 2048], P(None, 'rows'), may hold values from 0 to 1
- inv_length: float32 [22], replicated, may hold values from 0.4 to 2
- grid_coords: int32 [22, 262144], P(None, 'cand'), may hold values from 0 to 20
- frequencies: float32 [22, 8192], P(None, 'rows'), may hold values from -8 to 8
- phases: float32 [8192], P('rows'), may hold values from -3.140625 to 3.140625
- prior_coef: bfloat16 [256, 8192], P('cand', 'rows'), may hold values from -6 to 6
Outputs:
- samples_at: float32 [262144, 256], P('cand', 'rows')
Inputs may be any that keep to these rules, and one draw needn't show every extreme that they name: `factor_rows`: entries in and above the diagonal blocks of 512 x 512 are zero. `diag_inv`: each block of 512 rows is lower triangular with a positive diagonal.
All inputs are finite; a program needn't handle non-finite values.
Results may differ from a plain program's by a relative error of at most 0.004.
Values may be sent and summed in bfloat16 or wider, within the bound.
No kernel may reach another device: no remote copies, remote signals or barrier semaphores. Data moves between devices by JAX's collectives and lax.ppermute only.
A program may use at most 320 MiB of HBM per device.

v0:
```python
import jax
import jax.numpy as jnp
from jax import lax
from jax.sharding import PartitionSpec as P

FEAT = 8192
GRID = 21


def from_behind(shard, axis, by):
    peers = lax.axis_size(axis)
    pairs = [(i, i + by) for i in range(peers) if 0 <= i + by < peers]
    return lax.ppermute(shard, axis, pairs)


def solve_chain(whitened, factor_rows, diag_inv):
    sections = lax.axis_size("rows")
    position = lax.axis_index("rows")
    rows_dev = factor_rows.shape[0]
    block_width = diag_inv.shape[1]
    offset = position * rows_dev
    carried = jnp.zeros((whitened.shape[0], factor_rows.shape[1]), jnp.float32)
    weights = jnp.zeros_like(whitened)

    def solve_own(state):
        incoming, earlier = state
        remaining = whitened - lax.dynamic_slice_in_dim(incoming, offset, rows_dev, 1)
        pieces = []
        for block_id in reversed(range(rows_dev // block_width)):
            first_col = block_id * block_width
            solved = jnp.dot(
                remaining[:, first_col : first_col + block_width],
                diag_inv,
                precision=lax.Precision.HIGHEST,
                preferred_element_type=jnp.float32,
            )
            own_columns = lax.dynamic_slice_in_dim(factor_rows, offset, rows_dev, 1)
            remaining = remaining - jnp.dot(
                solved,
                own_columns,
                precision=lax.Precision.HIGHEST,
                preferred_element_type=jnp.float32,
            )
            pieces.append(solved)
        solved_all = jnp.concatenate(pieces[::-1], axis=1)
        updated = incoming + jnp.dot(
            solved_all,
            factor_rows,
            precision=lax.Precision.HIGHEST,
            preferred_element_type=jnp.float32,
        )
        return (updated, solved_all)

    def pass_on(state):
        return state

    for section_id in range(sections):
        carried, weights = lax.cond(
            position == sections - 1 - section_id, solve_own, pass_on, (carried, weights)
        )
        if section_id + 1 < sections:
            carried = from_behind(carried, "rows", -1)
    return weights


def prior_slab(mixture, frequencies, phases, coef_slab):
    angles = (
        lax.dot_general(
            mixture,
            frequencies,
            (((0,), (0,)), ((), ())),
            precision=lax.Precision.HIGHEST,
            preferred_element_type=jnp.float32,
        )
        + phases[None, :]
    )
    features_map = (jnp.sqrt(2.0 / FEAT) * jnp.cos(angles)).astype(jnp.bfloat16)
    return lax.dot_general(
        features_map, coef_slab, (((1,), (1,)), ((), ())), preferred_element_type=jnp.float32
    )


def cross_part(mixture, observed, inv_length, weights_wire):
    squared = jnp.zeros((mixture.shape[1], observed.shape[1]), jnp.float32)
    for column in range(mixture.shape[0]):
        gap = (mixture[column][:, None] - observed[column][None, :]) * inv_length[column]
        squared = squared + gap * gap
    kernel_tile = jnp.exp(-0.5 * squared).astype(jnp.bfloat16)
    return lax.dot_general(
        kernel_tile, weights_wire, (((1,), (1,)), ((), ())), preferred_element_type=jnp.float32
    )


def body(
    whitened,
    factor_rows,
    diag_inv,
    observed,
    inv_length,
    grid_coords,
    frequencies,
    phases,
    prior_coef,
):
    coef_all = lax.all_gather(prior_coef, "cand", axis=0, tiled=True)
    weights = lax.all_gather(
        solve_chain(whitened, factor_rows, diag_inv).astype(jnp.bfloat16),
        "cand",
        axis=0,
        tiled=True,
    )
    mixture = grid_coords.astype(jnp.float32) / (GRID - 1)
    summed = prior_slab(mixture, frequencies, phases, coef_all) + cross_part(
        mixture, observed, inv_length, weights
    )
    return lax.psum_scatter(summed, "rows", scatter_dimension=1, tiled=True)


def solution(mesh):
    in_specs = (
        P("cand", "rows"),
        P("rows", None),
        P("rows", None),
        P(None, "rows"),
        P(),
        P(None, "cand"),
        P(None, "rows"),
        P("rows"),
        P("cand", "rows"),
    )
    out_specs = P("cand", "rows")
    return jax.shard_map(body, mesh=mesh, in_specs=in_specs, out_specs=out_specs, check_vma=False)
```

profile of v0, /device:TPU:1, one launch (start us, length us, event | category | flops | bytes accessed | tf_op | source)
XLA Modules:
  0.0 327.4 jit_solution(7780740695992511488)
XLA Ops:
  6.5 0.7 all-gather.4.cloned.1.call-update
  7.3 0.0 reduce-scatter.2.cloned.1.call-start
  7.3 0.6 conditional.4
  7.3 0.6 broadcast_in_dim.6
  7.9 1.3 collective-permute-start
  9.2 1.0 convert_multiply_fusion
  10.3 0.3 fusion.85
  10.6 0.8 fusion.88
  11.4 1.2 fusion.87
  12.6 2.1 fusion.89
  14.6 1.4 fusion.90
  16.1 1.3 collective-permute-start.1
  17.4 44.7 %exponential_convert_fusion.4 = bf16[4096,512]{1,0:T(8,128)(2,1)} fusion(f32[]{:T(128)} %bitcast.66, f32[512]{0:T(512)S(1)} %bitcast.129, f32[4096]{0:T(1024)S(1)} %bitcast.107, f32[]{:T(128)} %bitcast.63, f32[512]{0:T(512)S(1)} %bitcast.130, f32[4096]{0:T(1024)S(1)} %bitcast.87, f32[]{:T(128)} %bitcast.60, f32[512]{0:T(512)S(1)} %bitcast.110, ...), kind=kLoop, calls=%fused_computation.18.clone.clone.1 | loop fusion | flops 186646528 | bytes 4599896 | tf_op jit(solution)/shard_map/dot_general | solution.py:89
  62.1 1.6 collective-permute-start.2
  63.7 30.3 %fusion.84 = f32[4096,2048]{1,0:T(8,128)} fusion(f32[22,2048]{1,0:T(8,128)S(1)} %copy-done, s32[22,4096]{1,0:T(8,128)S(1)} %copy-done.3), kind=kOutput, calls=%fused_computation.91 | convolution fusion | flops 2214772736 | bytes 34095104 | tf_op jit(solution)/shard_map/dot_general | solution.py:68
  94.0 1.2 conditional.7
  94.0 1.2 fusion.8
  95.3 0.7 convert_bitcast_fusion
  96.0 48.9 %all-gather.1 = bf16[64,4,512]{2,1,0:T(4,128)(2,1)S(1)} all-gather(bf16[1,4,512]{2,1,0:T(4,128)(2,1)S(1)} %convert_bitcast_fusion), channel_id=1, replica_groups=mesh['rows'=4,'cand'=64] {'cand'}, dimensions={0}, use_global_device_ids=true | all-gather | bytes 266240 | tf_op jit(solution)/shard_map/all_gather | solution.py:106
  144.8 0.1 reshape.26
  144.9 1.3 reshape.24
  146.3 114.3 %fusion.12 = f32[4096,256]{0,1:T(8,128)S(1)} fusion(bf16[256,2048]{1,0:T(8,128)(2,1)S(1)} %reshape.24, f32[4096,2048]{1,0:T(8,128)} %fusion.84, f32[2048]{0:T(1024)S(1)} %copy-done.5), kind=kOutput, calls=%fused_computation.15 | convolution fusion | flops 4320133120 | bytes 38805504 | tf_op jit(solution)/shard_map/dot_general | solution.py:78
  260.6 3.4 %convolution_add_fusion.2 = f32[4096,256]{0,1:T(8,128)} fusion(f32[4096,256]{0,1:T(8,128)S(1)} %fusion.12, bf16[256,512]{1,0:T(8,128)(2,1)S(1)} %reshape.26, bf16[4096,512]{1,0:T(8,128)(2,1)S(1)} %copy-done.1), kind=kOutput, calls=%fused_computation.19 | convolution fusion | flops 1074790400 | bytes 12845056 | tf_op jit(solution)/shard_map/dot_general | solution.py:89
  264.0 56.5 %reduce-scatter.2.cloned.1.call-done = f32[4096,64]{0,1:T(8,128)} async-done(((f32[4096,256]{0,1:T(8,128)}), f32[4096,64]{0,1:T(8,128)}) %reduce-scatter.2.cloned.1.call-update) | async-done | bytes 1048592 | tf_op jit(solution)/shard_map/reduce_scatter | solution.py:116
  (22 shorter events, 0.1 us)
Async XLA Ops:
  6.5 57.1 %copy-start = (f32[22,2048]{1,0:T(8,128)S(1)}, f32[22,2048]{1,0:T(8,128)}, u32[]{:S(2)}) copy-start(f32[22,2048]{1,0:T(8,128)} %param.23) | copy-start | bytes 540676
  6.5 138.4 %all-gather.4.cloned.1.call-start = ((), (), s32[]{:S(2)}) async-start(), calls=%async_computation.2 | async-start | bytes 1064960 | tf_op jit(solution)/shard_map/all_gather | solution.py:105
  7.3 313.3 %reduce-scatter.2.cloned.1.call-start = ((), (), s32[]{:S(2)}) async-start(), calls=%async_computation.1 | async-start | bytes 5242880 | tf_op jit(solution)/shard_map/reduce_scatter | solution.py:116
  7.9 8.1 %collective-permute-start = (f32[4,2048]{1,0:T(4,128)S(1)}, f32[4,2048]{1,0:T(4,128)S(1)}, u32[]{:S(2)}, u32[]{:S(2)}) collective-permute-start(f32[4,2048]{1,0:T(4,128)S(1)} %get-tuple-element.77), channel_id=1, source_target_pairs={{64,0},{128,64},{192,128},{65,1},{129,65},{193,129},{66,2},{130,66... | collective-permute-start | bytes 98312 | tf_op jit(solution)/shard_map/ppermute | solution.py:13
  10.3 53.4 %copy-start.3 = (s32[22,4096]{1,0:T(8,128)S(1)}, s32[22,4096]{1,0:T(8,128)}, u32[]{:S(2)}) copy-start(s32[22,4096]{1,0:T(8,128)} %param.22) | copy-start | bytes 1081348
  16.1 45.9 %collective-permute-start.1 = (f32[4,2048]{1,0:T(4,128)S(1)}, f32[4,2048]{1,0:T(4,128)S(1)}, u32[]{:S(2)}, u32[]{:S(2)}) collective-permute-start(f32[4,2048]{1,0:T(4,128)S(1)} %get-tuple-element.79), channel_id=1, source_target_pairs={{64,0},{128,64},{192,128},{65,1},{129,65},{193,129},{66,2},{130,66... | collective-permute-start | bytes 98312 | tf_op jit(solution)/shard_map/ppermute | solution.py:13
  62.0 32.0 %copy-start.2 = (f32[512,512]{1,0:T(8,128)S(1)}, f32[512,512]{1,0:T(8,128)}, u32[]{:S(2)}) copy-start(f32[512,512]{1,0:T(8,128)} %param.19) | copy-start | bytes 3145732
  62.0 32.0 %copy-start.4 = (f32[4,512]{1,0:T(4,128)S(1)}, f32[4,512]{1,0:T(4,128)}, u32[]{:S(2)}) copy-start(f32[4,512]{1,0:T(4,128)} %param.17) | copy-start | bytes 24580
  62.0 84.2 %copy-start.5 = (f32[2048]{0:T(1024)S(1)}, f32[2048]{0:T(1024)}, u32[]{:S(2)}) copy-start(f32[2048]{0:T(1024)} %param.24) | copy-start | bytes 24580
  62.1 32.0 %collective-permute-start.2 = (f32[4,2048]{1,0:T(4,128)S(1)}, f32[4,2048]{1,0:T(4,128)S(1)}, u32[]{:S(2)}, u32[]{:S(2)}) collective-permute-start(f32[4,2048]{1,0:T(4,128)S(1)} %get-tuple-element.82), channel_id=1, source_target_pairs={{64,0},{128,64},{192,128},{65,1},{129,65},{193,129},{66,2},{130,66... | collective-permute-start | bytes 98312 | tf_op jit(solution)/shard_map/ppermute | solution.py:13
  146.3 114.3 %copy-start.1 = (bf16[4096,512]{1,0:T(8,128)(2,1)S(1)}, bf16[4096,512]{1,0:T(8,128)(2,1)}, u32[]{:S(2)}) copy-start(bf16[4096,512]{1,0:T(8,128)(2,1)} %exponential_convert_fusion.4) | copy-start | bytes 12582916
Sparse Core Ops, SparseCore 0:
  10.1 80.9 all-gather.3
  264.1 56.3 reduce-scatter.1
where the time goes:
time: 328 us; the launch traced here: 327 us
  matrix products  149 us (45%)
  waiting for transfers between devices  57.3 us (17%)
  blocking collectives  48.9 us (15%)
  other arithmetic  46.4 us (14%)
  between operations  13.6 us (4%)
  local copies, waits for them, and re-layouts  7.82 us (2%)
  starting transfers between devices  4.21 us (1%)
    dot_general x1, matrix products, prior_slab(): lax.dot_general(features_map, coef_slab, (((1,), (1,)), ((), ())), prefer...  114 us
    reduce_scatter x1, waiting for transfers between devices, body(): return lax.psum_scatter(summed, 'rows', scatter_dimension=1, tiled=True)  56.5 us
    all_gather x1, blocking collectives, body(): lax.all_gather(solve_chain(whitened, factor_rows, diag_inv).astype(jnp.bf...  48.9 us
    dot_general x1, other arithmetic, cross_part(): lax.dot_general(kernel_tile, weights_wire, (((1,), (1,)), ((), ())), pref...  44.7 us
    dot_general x1, matrix products, prior_slab(): lax.dot_general(mixture, frequencies, (((0,), (0,)), ((), ())), precision...  30.3 us
  transfers between devices with their start and end apart: 5, of which 1 were waited for; matrix products, arithmetic and copies ran while one was open for 26% of the time, Pallas kernels for 0%

commit v1 on v0

--- a/solution.py
+++ b/solution.py
@@ -103,11 +103,17 @@
     prior_coef,
 ):
     coef_all = lax.all_gather(prior_coef, "cand", axis=0, tiled=True)
-    weights = lax.all_gather(
-        solve_chain(whitened, factor_rows, diag_inv).astype(jnp.bfloat16),
-        "cand",
+    weights = jnp.concatenate(
+        lax.all_to_all(
+            jnp.stack(
+                [solve_chain(whitened, factor_rows, diag_inv).astype(jnp.bfloat16)]
+                * lax.axis_size("cand")
+            ),
+            "cand",
+            0,
+            0,
+        ),
         axis=0,
-        tiled=True,
     )
     mixture = grid_coords.astype(jnp.float32) / (GRID - 1)
     summed = prior_slab(mixture, frequencies, phases, coef_all) + cross_part(

time: 328 us -> 307 us (0.936)
  blocking collectives: 48.9 us -> 0 us
  starting transfers between devices: 4.21 us -> 17.7 us
  waiting for transfers between devices: 57.3 us -> 70.2 us
    all_gather x1 -> x0, blocking collectives: 48.9 us -> none  [body(): lax.all_gather(solve_chain(whitened, factor_rows, diag_inv).astype(jnp.bf...]
    all_to_all x0 -> x1, starting transfers between devices: none -> 13.7 us  [body(): lax.all_to_all(jnp.stack([solve_chain(whitened, factor_rows, diag_inv).as...]
    reduce_scatter x1, waiting for transfers between devices: 56.5 us -> 65.4 us  [body(): return lax.psum_scatter(summed, 'rows', scatter_dimension=1, tiled=True)]
    ppermute x3, waiting for transfers between devices: 0.01 us -> 4 us  [from_behind(): return lax.ppermute(shard, axis, pairs)]
  transfers between devices with their start and end apart: 5 -> 6, of which waited for: 1 -> 2; matrix products, arithmetic and copies ran while one was open for 26% -> 28% of each run, Pallas kernels for 0% -> 0%
where the time goes in v1:
time: 307 us; the launch traced here: 306 us
  matrix products  150 us (49%)
  waiting for transfers between devices  70.2 us (23%)
  other arithmetic  46.4 us (15%)
  starting transfers between devices  17.7 us (6%)
  between operations  13.6 us (4%)
  local copies, waits for them, and re-layouts  7.78 us (3%)
    dot_general x1, matrix products, prior_slab(): lax.dot_general(features_map, coef_slab, (((1,), (1,)), ((), ())), prefer...  114 us
    reduce_scatter x1, waiting for transfers between devices, body(): return lax.psum_scatter(summed, 'rows', scatter_dimension=1, tiled=True)  65.4 us
    dot_general x1, other arithmetic, cross_part(): lax.dot_general(kernel_tile, weights_wire, (((1,), (1,)), ((), ())), pref...  44.6 us
    dot_general x1, matrix products, prior_slab(): lax.dot_general(mixture, frequencies, (((0,), (0,)), ((), ())), precision...  30.2 us
    all_to_all x1, starting transfers between devices, body(): lax.all_to_all(jnp.stack([solve_chain(whitened, factor_rows, diag_inv).as...  13.7 us
  transfers between devices with their start and end apart: 6, of which 2 were waited for; matrix products, arithmetic and copies ran while one was open for 28% of the time, Pallas kernels for 0%

profile of v1, /device:TPU:1, one launch (start us, length us, event | category | flops | bytes accessed | tf_op | source)
XLA Modules:
  0.0 306.0 jit_solution(5156806620968819691)
XLA Ops:
  6.5 0.7 all-gather.3.cloned.1.call-update
  7.3 0.6 conditional.4
  7.3 0.6 broadcast_in_dim.6
  7.9 1.3 collective-permute-start
  9.2 1.0 convert_multiply_fusion
  10.3 0.3 fusion.85
  10.6 0.8 fusion.88
  11.4 1.2 fusion.87
  12.5 2.0 fusion.89
  14.6 1.4 collective-permute-start.1
  16.1 0.6 fusion.90
  16.7 4.0 %collective-permute-done.1 = f32[4,2048]{1,0:T(4,128)S(1)} collective-permute-done((f32[4,2048]{1,0:T(4,128)S(1)}, f32[4,2048]{1,0:T(4,128)S(1)}, u32[]{:S(2)}, u32[]{:S(2)}) %collective-permute-start.1) | collective-permute-done | bytes 32800 | tf_op jit(solution)/shard_map/ppermute | solution.py:13
  20.7 1.3 collective-permute-start.2
  22.0 44.6 %exponential_convert_fusion.4 = bf16[4096,512]{1,0:T(8,128)(2,1)} fusion(f32[]{:T(128)} %bitcast.66, f32[512]{0:T(512)S(1)} %bitcast.127, f32[4096]{0:T(1024)S(1)} %bitcast.105, f32[]{:T(128)} %bitcast.63, f32[512]{0:T(512)S(1)} %bitcast.128, f32[4096]{0:T(1024)S(1)} %bitcast.85, f32[]{:T(128)} %bitcast.60, f32[512]{0:T(512)S(1)} %bitcast.108, ...), kind=kLoop, calls=%fused_computation.18.clone.clone.1 | loop fusion | flops 186646528 | bytes 4599896 | tf_op jit(solution)/shard_map/dot_general | solution.py:89
  66.6 2.5 conditional.7
  66.6 2.5 fusion.8
  69.1 0.7 convert_element_type.31
  69.8 0.8 stack.2
  70.5 13.7 %all-to-all-start = ((bf16[64,4,512]{2,1,0:T(4,128)(2,1)}), bf16[64,4,512]{2,1,0:T(4,128)(2,1)S(1)}, u32[]{:S(2)}, u32[]{:S(2)}) async-start(bf16[64,4,512]{2,1,0:T(4,128)(2,1)} %stack.2), calls=%async_computation | async-start | bytes 524288 | tf_op jit(solution)/shard_map/all_to_all | solution.py:107
  84.3 30.2 %fusion.84 = f32[4096,2048]{1,0:T(8,128)} fusion(f32[22,2048]{1,0:T(8,128)S(1)} %copy-done, s32[22,4096]{1,0:T(8,128)S(1)} %copy-done.2), kind=kOutput, calls=%fused_computation.90 | convolution fusion | flops 2214772736 | bytes 34095104 | tf_op jit(solution)/shard_map/dot_general | solution.py:68
  114.6 1.3 reshape.30
  115.9 114.4 %fusion.12 = f32[4096,256]{0,1:T(8,128)S(1)} fusion(bf16[256,2048]{1,0:T(8,128)(2,1)S(1)} %reshape.30, f32[4096,2048]{1,0:T(8,128)} %fusion.84, f32[2048]{0:T(1024)S(1)} %copy-done.4), kind=kOutput, calls=%fused_computation.15 | convolution fusion | flops 4320133120 | bytes 38805504 | tf_op jit(solution)/shard_map/dot_general | solution.py:78
  230.3 3.4 %convolution_add_fusion.2 = f32[4096,256]{0,1:T(8,128)} fusion(f32[4096,256]{0,1:T(8,128)S(1)} %fusion.12, bf16[256,512]{1,0:T(8,128)(2,1)S(1)} %reshape.28, bf16[4096,512]{1,0:T(8,128)(2,1)S(1)} %copy-done.1), kind=kOutput, calls=%fused_computation.19 | convolution fusion | flops 1074790400 | bytes 12845056 | tf_op jit(solution)/shard_map/dot_general | solution.py:89
  233.8 65.4 %reduce-scatter.2.cloned.1.call-done = f32[4096,64]{0,1:T(8,128)} async-done(((f32[4096,256]{0,1:T(8,128)}), f32[4096,64]{0,1:T(8,128)}) %reduce-scatter.2.cloned.1.call-update) | async-done | bytes 1048592 | tf_op jit(solution)/shard_map/reduce_scatter | solution.py:122
  (22 shorter events, 0.2 us)
Async XLA Ops:
  6.5 77.7 %copy-start = (f32[22,2048]{1,0:T(8,128)S(1)}, f32[22,2048]{1,0:T(8,128)}, u32[]{:S(2)}) copy-start(f32[22,2048]{1,0:T(8,128)} %param.23) | copy-start | bytes 540676
  6.5 9.5 %copy-start.3 = (f32[22]{0:T(128)S(1)}, f32[22]{0:T(128)}, u32[]{:S(2)}) copy-start(f32[22]{0:T(128)} %param.21) | copy-start | bytes 268
  6.5 108.0 %all-gather.3.cloned.1.call-start = ((), (), s32[]{:S(2)}) async-start(), calls=%async_computation.3 | async-start | bytes 1064960 | tf_op jit(solution)/shard_map/all_gather | solution.py:105
  7.9 6.7 %collective-permute-start = (f32[4,2048]{1,0:T(4,128)S(1)}, f32[4,2048]{1,0:T(4,128)S(1)}, u32[]{:S(2)}, u32[]{:S(2)}) collective-permute-start(f32[4,2048]{1,0:T(4,128)S(1)} %get-tuple-element.77), channel_id=1, source_target_pairs={{64,0},{128,64},{192,128},{65,1},{129,65},{193,129},{66,2},{130,66... | collective-permute-start | bytes 98312 | tf_op jit(solution)/shard_map/ppermute | solution.py:13
  14.6 69.7 %copy-start.2 = (s32[22,4096]{1,0:T(8,128)S(1)}, s32[22,4096]{1,0:T(8,128)}, u32[]{:S(2)}) copy-start(s32[22,4096]{1,0:T(8,128)} %param.22) | copy-start | bytes 1081348
  14.6 6.1 %collective-permute-start.1 = (f32[4,2048]{1,0:T(4,128)S(1)}, f32[4,2048]{1,0:T(4,128)S(1)}, u32[]{:S(2)}, u32[]{:S(2)}) collective-permute-start(f32[4,2048]{1,0:T(4,128)S(1)} %get-tuple-element.79), channel_id=1, source_target_pairs={{64,0},{128,64},{192,128},{65,1},{129,65},{193,129},{66,2},{130,66... | collective-permute-start | bytes 98312 | tf_op jit(solution)/shard_map/ppermute | solution.py:13
  20.7 45.9 %collective-permute-start.2 = (f32[4,2048]{1,0:T(4,128)S(1)}, f32[4,2048]{1,0:T(4,128)S(1)}, u32[]{:S(2)}, u32[]{:S(2)}) collective-permute-start(f32[4,2048]{1,0:T(4,128)S(1)} %get-tuple-element.82), channel_id=1, source_target_pairs={{64,0},{128,64},{192,128},{65,1},{129,65},{193,129},{66,2},{130,66... | collective-permute-start | bytes 98312 | tf_op jit(solution)/shard_map/ppermute | solution.py:13
  70.5 43.9 %all-to-all-start = ((bf16[64,4,512]{2,1,0:T(4,128)(2,1)}), bf16[64,4,512]{2,1,0:T(4,128)(2,1)S(1)}, u32[]{:S(2)}, u32[]{:S(2)}) async-start(bf16[64,4,512]{2,1,0:T(4,128)(2,1)} %stack.2), calls=%async_computation | async-start | bytes 524288 | tf_op jit(solution)/shard_map/all_to_all | solution.py:107
  84.2 31.7 %copy-start.4 = (f32[2048]{0:T(1024)S(1)}, f32[2048]{0:T(1024)}, u32[]{:S(2)}) copy-start(f32[2048]{0:T(1024)} %param.24) | copy-start | bytes 24580
  84.2 215.0 %reduce-scatter.2.cloned.1.call-start = ((), (), s32[]{:S(2)}) async-start(), calls=%async_computation.2 | async-start | bytes 5242880 | tf_op jit(solution)/shard_map/reduce_scatter | solution.py:122
  115.9 114.4 %copy-start.1 = (bf16[4096,512]{1,0:T(8,128)(2,1)S(1)}, bf16[4096,512]{1,0:T(8,128)(2,1)}, u32[]{:S(2)}) copy-start(bf16[4096,512]{1,0:T(8,128)(2,1)} %exponential_convert_fusion.4) | copy-start | bytes 12582916
Sparse Core Ops, SparseCore 0:
  10.1 81.3 all-gather.2
  233.9 65.2 reduce-scatter.1
